TPU v7x, 32 devices: a whole 2x2x4 slice. The times are simulated.
32 devices in a mesh: dp: 8 (over z, core), row: 2 (over x), col: 2 (over y).
Axes of the slice: x: 2, y: 2, z: 4, core: 2. Of those that a mesh axis runs over, the one named last changes fastest.
Arguments:
- tokens: bfloat16 [16384, 1024], P(('dp', 'row'), 'col'), may hold values from -6 to 6
- mixer_gain: float32 [1024], P('col'), may hold values from 0.1 to 1.9
- in_weight: bfloat16 [1024, 3, 1024], P('col', None, 'row'), may hold values from -0.1875 to 0.1875
- conv_kernel: float32 [3, 1024], P(None, 'row'), may hold values from -3.5 to 3.5
- out_weight: bfloat16 [1024, 1024], P('row', 'col'), may hold values from -0.1875 to 0.1875
- ffn_gain: float32 [1024], P('col'), may hold values from 0.1 to 1.9
- ffn_weight: bfloat16 [1024, 2, 4608], P('col', None, 'row'), may hold values from -0.1875 to 0.1875
- down_weight: bfloat16 [4608, 1024], P('row', 'col'), may hold values from -0.1875 to 0.1875
- cotangent: bfloat16 [16384, 1024], P(('dp', 'row'), 'col'), may hold values from -6 to 6
Outputs:
- output: bfloat16 [16384, 1024], P(('dp', 'row'), 'col')
- d_tokens: float32 [16384, 1024], P(('dp', 'row'), 'col')
- d_mixer_gain: float32 [1024], P('col')
- d_in_weight: float32 [1024, 3, 1024], P('col', None, 'row')
- d_conv_kernel: float32 [3, 1024], P(None, 'row')
- d_out_weight: float32 [1024, 1024], P('row', 'col')
- d_ffn_gain: float32 [1024], P('col')
- d_ffn_weight: float32 [1024, 2, 4608], P('col', None, 'row')
- d_down_weight: float32 [4608, 1024], P('row', 'col')
All inputs are finite; a program needn't handle non-finite values.
Results may differ from a plain program's by a relative error of at most 0.015.
Values may be sent and summed in bfloat16 or wider, within the bound.
No kernel may reach another device: no remote copies, remote signals or barrier semaphores. Data moves between devices by JAX's collectives and lax.ppermute only.
A program may use at most 320 MiB of HBM per device.

v0:
```python
import jax
import jax.numpy as jnp
from jax import lax
from jax.sharding import PartitionSpec as P

D = 1024
EPS = 1e-05


def shifted(block, axis, distance):
    devices = range(lax.axis_size(axis))
    route = [(i - distance, i) for i in devices if i - distance in devices]
    return lax.ppermute(block, axis, route)


def dense(left, matrix, transposed):
    if transposed:
        return lax.dot_general(
            left, matrix, (((1,), (1,)), ((), ())), preferred_element_type=jnp.float32
        )
    return jnp.dot(left, matrix, preferred_element_type=jnp.float32)


def grads_of(left, right):
    return lax.dot_general(
        left, right, (((0,), (0,)), ((), ())), preferred_element_type=jnp.float32
    )


def tokens_by_row(value):
    return lax.all_gather(value, "row", axis=0, tiled=True)


def tokens_by_col(value):
    return lax.all_gather(value, "col", axis=0, tiled=True)


def spread_wide(gathered, matrix, transposed):
    height = gathered.shape[0] // lax.axis_size("col")

    def partial_rows(start, count):
        return dense(gathered, matrix, transposed)

    return lax.psum_scatter(
        partial_rows(jnp.int32(0), height * lax.axis_size("col")),
        "col",
        scatter_dimension=0,
        tiled=True,
    )


def spread_narrow(gathered, matrix, transposed):
    height = gathered.shape[0] // lax.axis_size("row")

    def partial_rows(start, count):
        return dense(gathered, matrix, transposed)

    return lax.psum_scatter(
        partial_rows(jnp.int32(0), height * lax.axis_size("row")),
        "row",
        scatter_dimension=0,
        tiled=True,
    )


def width_total(value):
    return lax.psum(value, "col")


def local(
    tokens,
    mixer_gain,
    in_weight,
    conv_kernel,
    out_weight,
    ffn_gain,
    ffn_weight,
    down_weight,
    cotangent,
):
    xfloat = tokens.astype(jnp.float32)
    scale_one = lax.rsqrt(width_total(jnp.sum(xfloat * xfloat, axis=1, keepdims=True)) / D + EPS)
    normed_one = xfloat * scale_one
    hidden_one = (normed_one * mixer_gain).astype(jnp.bfloat16)
    wide_in = in_weight.reshape(in_weight.shape[0], -1)
    gathered_one = tokens_by_row(hidden_one)
    projected = spread_wide(gathered_one, wide_in, False)
    block_width = conv_kernel.shape[1]
    gate_b = projected[:, :block_width]
    gate_c = projected[:, block_width : 2 * block_width]
    values = projected[:, 2 * block_width :]
    mixed_in = gate_b * values
    previous = shifted(mixed_in[-2:], "col", 1)
    extended = jnp.concatenate([previous, mixed_in], 0)
    lag_one = extended[1:-1]
    lag_two = extended[:-2]
    convolved = conv_kernel[2] * mixed_in + conv_kernel[1] * lag_one + conv_kernel[0] * lag_two
    mixer_out = (gate_c * convolved).astype(jnp.bfloat16)
    gathered_mix = tokens_by_col(mixer_out)
    residual = xfloat + spread_narrow(gathered_mix, out_weight, False)
    scale_two = lax.rsqrt(
        width_total(jnp.sum(residual * residual, axis=1, keepdims=True)) / D + EPS
    )
    normed_two = residual * scale_two
    hidden_two = (normed_two * ffn_gain).astype(jnp.bfloat16)
    wide_ffn = ffn_weight.reshape(ffn_weight.shape[0], -1)
    gathered_two = tokens_by_row(hidden_two)
    gate_up = spread_wide(gathered_two, wide_ffn, False)
    inner_width = down_weight.shape[0]
    gate_part = gate_up[:, :inner_width]
    up_part = gate_up[:, inner_width:]
    sigmoid_gate = jax.nn.sigmoid(gate_part)
    activated = (gate_part * sigmoid_gate * up_part).astype(jnp.bfloat16)
    gathered_act = tokens_by_col(activated)
    output = (residual + spread_narrow(gathered_act, down_weight, False)).astype(jnp.bfloat16)
    cot_rows = tokens_by_row(cotangent)
    d_act = spread_wide(cot_rows, down_weight, True)
    grad_down = grads_of(gathered_act, cot_rows)
    d_gate = d_act * up_part * sigmoid_gate * (1.0 + gate_part * (1.0 - sigmoid_gate))
    d_up = d_act * gate_part * sigmoid_gate
    d_gate_up = jnp.concatenate([d_gate, d_up], 1).astype(jnp.bfloat16)
    dgu_rows = tokens_by_col(d_gate_up)
    d_hidden_two = spread_narrow(dgu_rows, wide_ffn, True)
    grad_ffn = grads_of(gathered_two, dgu_rows).reshape(ffn_weight.shape)
    scaled_two = d_hidden_two * ffn_gain
    inner_two = width_total(jnp.sum(scaled_two * normed_two, axis=1, keepdims=True)) / D
    d_residual = cotangent.astype(jnp.float32) + scale_two * (scaled_two - normed_two * inner_two)
    gain_two_part = jnp.sum(d_hidden_two * normed_two, axis=0)
    d_residual_b = d_residual.astype(jnp.bfloat16)
    dres_rows = tokens_by_row(d_residual_b)
    d_mix = spread_wide(dres_rows, out_weight, True)
    grad_out = grads_of(gathered_mix, dres_rows)
    d_gate_c = d_mix * convolved
    d_conv = d_mix * gate_c
    following = shifted(d_conv[:2], "col", -1)
    ahead_rows = jnp.concatenate([d_conv, following], 0)
    d_mixed = (
        conv_kernel[2] * d_conv
        + conv_kernel[1] * ahead_rows[1:-1]
        + conv_kernel[0] * ahead_rows[2:]
    )
    kernel_part = jnp.stack(
        [
            jnp.sum(d_conv * lag_two, axis=0),
            jnp.sum(d_conv * lag_one, axis=0),
            jnp.sum(d_conv * mixed_in, axis=0),
        ]
    )
    d_projected = jnp.concatenate([d_mixed * values, d_gate_c, d_mixed * gate_b], 1).astype(
        jnp.bfloat16
    )
    dproj_rows = tokens_by_col(d_projected)
    d_hidden_one = spread_narrow(dproj_rows, wide_in, True)
    grad_in = grads_of(gathered_one, dproj_rows).reshape(in_weight.shape)
    scaled_one = d_hidden_one * mixer_gain
    inner_one = width_total(jnp.sum(scaled_one * normed_one, axis=1, keepdims=True)) / D
    d_tokens = d_residual + scale_one * (scaled_one - normed_one * inner_one)
    gain_one_part = jnp.sum(d_hidden_one * normed_one, axis=0)
    grad_in, grad_out, grad_ffn, grad_down = (
        lax.psum(grad_in.astype(jnp.bfloat16), "dp").astype(jnp.float32),
        lax.psum(grad_out.astype(jnp.bfloat16), "dp").astype(jnp.float32),
        lax.psum(grad_ffn.astype(jnp.bfloat16), "dp").astype(jnp.float32),
        lax.psum(grad_down.astype(jnp.bfloat16), "dp").astype(jnp.float32),
    )
    gain_width = mixer_gain.shape[0]
    col_offset = lax.axis_index("col") * gain_width
    row_offset = lax.axis_index("row") * block_width
    zero_index = jnp.zeros((), jnp.int32)
    full_one = lax.dynamic_update_slice(jnp.zeros((D,), jnp.float32), gain_one_part, (col_offset,))
    full_two = lax.dynamic_update_slice(jnp.zeros((D,), jnp.float32), gain_two_part, (col_offset,))
    full_kernel = lax.dynamic_update_slice(
        jnp.zeros((3, D), jnp.float32), kernel_part, (zero_index, row_offset)
    )
    total_one, total_two, total_kernel = lax.psum(
        (full_one, full_two, full_kernel), ("dp", "row", "col")
    )
    grad_gain_one = lax.dynamic_slice_in_dim(total_one, col_offset, gain_width, 0)
    grad_gain_two = lax.dynamic_slice_in_dim(total_two, col_offset, gain_width, 0)
    grad_kernel = lax.dynamic_slice_in_dim(total_kernel, row_offset, block_width, 1)
    return (
        output,
        d_tokens,
        grad_gain_one,
        grad_in,
        grad_kernel,
        grad_out,
        grad_gain_two,
        grad_ffn,
        grad_down,
    )


def solution(mesh):
    in_specs = (
        P(("dp", "row"), "col"),
        P("col"),
        P("col", None, "row"),
        P(None, "row"),
        P("row", "col"),
        P("col"),
        P("col", None, "row"),
        P("row", "col"),
        P(("dp", "row"), "col"),
    )
    out_specs = (
        P(("dp", "row"), "col"),
        P(("dp", "row"), "col"),
        P("col"),
        P("col", None, "row"),
        P(None, "row"),
        P("row", "col"),
        P("col"),
        P("col", None, "row"),
        P("row", "col"),
    )
    return jax.shard_map(local, mesh=mesh, in_specs=in_specs, out_specs=out_specs, check_vma=False)
```

profile of v0, /device:TPU:0, one launch (start us, length us, event | category | flops | bytes accessed | tf_op | source)
XLA Modules:
  0.0 1960.4 jit_solution(6422226700840039610)
XLA Ops:
  20.6 32.4 %all-gather.9.cloned.1.call-done = bf16[2048,512]{1,0:T(8,128)(2,1)} async-done(((bf16[1024,512]{1,0:T(8,128)(2,1)}), bf16[2048,512]{1,0:T(8,128)(2,1)}) %all-gather.9.cloned.1.call-update) | async-done | bytes 2097168 | tf_op jit(solution)/shard_map/all_gather | solution.py:31
  63.1 144.6 %reduce-scatter.9.cloned.1.call-done = f32[1024,1536]{1,0:T(8,128)} async-done(((f32[2048,1536]{1,0:T(8,128)}), f32[1024,1536]{1,0:T(8,128)}) %reduce-scatter.9.cloned.1.call-update) | async-done | bytes 6291472 | tf_op jit(solution)/shard_map/reduce_scatter | solution.py:44
  218.1 35.1 %all-gather.11.cloned.1.call-done = bf16[2048,512]{1,0:T(8,128)(2,1)} async-done(((bf16[1024,512]{1,0:T(8,128)(2,1)}), bf16[2048,512]{1,0:T(8,128)(2,1)}) %all-gather.11.cloned.1.call-update) | async-done | bytes 2097168 | tf_op jit(solution)/shard_map/all_gather | solution.py:35
  258.8 53.9 %reduce-scatter.11.cloned.1.call-done = f32[1024,512]{1,0:T(8,128)} async-done(((f32[2048,512]{1,0:T(8,128)}), f32[1024,512]{1,0:T(8,128)}) %reduce-scatter.11.cloned.1.call-update) | async-done | bytes 2097168 | tf_op jit(solution)/shard_map/reduce_scatter | solution.py:58
  324.0 23.2 %all-gather.17.cloned.1.call-done = bf16[2048,512]{1,0:T(8,128)(2,1)} async-done(((bf16[1024,512]{1,0:T(8,128)(2,1)}), bf16[2048,512]{1,0:T(8,128)(2,1)}) %all-gather.17.cloned.1.call-update) | async-done | bytes 2097168 | tf_op jit(solution)/shard_map/all_gather | solution.py:31
  347.2 11.5 fusion.24
  364.6 17.7 all-gather.13.cloned.1.call-done
  382.3 20.5 %fusion.22 = f32[2048,4608]{1,0:T(8,128)} fusion(bf16[2048,512]{1,0:T(8,128)(2,1)} %all-gather.13.cloned.1.call-done, bf16[512,4608]{1,0:T(8,128)(2,1)} %bitcast.44), kind=kOutput, calls=%fused_computation.62 | convolution fusion | flops 9663676416 | bytes 44564480 | tf_op jit(solution)/shard_map/dot_general | solution.py:21
  402.9 193.5 %reduce-scatter.17.cloned.1.call-done = f32[1024,2304]{1,0:T(8,128)} async-done(((f32[2048,2304]{1,0:T(8,128)}), f32[1024,2304]{1,0:T(8,128)}) %reduce-scatter.17.cloned.1.call-update) | async-done | bytes 9437200 | tf_op jit(solution)/shard_map/reduce_scatter | solution.py:44
  596.4 416.3 %reduce-scatter.13.cloned.1.call-done = f32[1024,4608]{1,0:T(8,128)} async-done(((f32[2048,4608]{1,0:T(8,128)}), f32[1024,4608]{1,0:T(8,128)}) %reduce-scatter.13.cloned.1.call-update) | async-done | bytes 18874384 | tf_op jit(solution)/shard_map/reduce_scatter | solution.py:44
  1012.7 13.4 multiply_convert_fusion.1
  1030.8 224.4 %all-gather.19.cloned.1.call-done = bf16[2048,4608]{1,0:T(8,128)(2,1)} async-done(((bf16[1024,4608]{1,0:T(8,128)(2,1)}), bf16[2048,4608]{1,0:T(8,128)(2,1)}) %all-gather.19.cloned.1.call-update) | async-done | bytes 18874384 | tf_op jit(solution)/shard_map/all_gather | solution.py:35
  1255.2 16.5 fusion.25
  1271.8 54.5 %reduce-scatter.19.cloned.1.call-done = f32[1024,512]{1,0:T(8,128)} async-done(((f32[2048,512]{1,0:T(8,128)}), f32[1024,512]{1,0:T(8,128)}) %reduce-scatter.19.cloned.1.call-update) | async-done | bytes 2097168 | tf_op jit(solution)/shard_map/reduce_scatter | solution.py:58
  1337.9 33.2 %all-gather.21.cloned.1.call-done = bf16[2048,512]{1,0:T(8,128)(2,1)} async-done(((bf16[1024,512]{1,0:T(8,128)(2,1)}), bf16[2048,512]{1,0:T(8,128)(2,1)}) %all-gather.21.cloned.1.call-update) | async-done | bytes 2097168 | tf_op jit(solution)/shard_map/all_gather | solution.py:31
  1376.9 53.7 %reduce-scatter.21.cloned.1.call-done = f32[1024,512]{1,0:T(8,128)} async-done(((f32[2048,512]{1,0:T(8,128)}), f32[1024,512]{1,0:T(8,128)}) %reduce-scatter.21.cloned.1.call-update) | async-done | bytes 2097168 | tf_op jit(solution)/shard_map/reduce_scatter | solution.py:44
  1448.3 101.9 %all-gather.15.cloned.1.call-done = bf16[2048,2304]{1,0:T(8,128)(2,1)} async-done(((bf16[1024,2304]{1,0:T(8,128)(2,1)}), bf16[2048,2304]{1,0:T(8,128)(2,1)}) %all-gather.15.cloned.1.call-update) | async-done | bytes 9437200 | tf_op jit(solution)/shard_map/all_gather | solution.py:35
  1550.2 10.5 convolution_convert_fusion.1
  1560.7 16.5 convolution_convert_fusion
  1588.7 43.9 %all-gather.23.cloned.1.call-done = bf16[2048,1536]{1,0:T(8,128)(2,1)} async-done(((bf16[1024,1536]{1,0:T(8,128)(2,1)}), bf16[2048,1536]{1,0:T(8,128)(2,1)}) %all-gather.23.cloned.1.call-update) | async-done | bytes 6291472 | tf_op jit(solution)/shard_map/all_gather | solution.py:35
  1652.2 10.4 fusion.23
  1662.9 170.8 %all-reduce.4.cloned.1.call-done = (bf16[512,3,512]{0,2,1:T(8,128)(2,1)}, bf16[512,512]{1,0:T(8,128)(2,1)}, bf16[512,2,2304]{2,1,0:T(2,128)(2,1)}, bf16[2304,512]{1,0:T(8,128)(2,1)}) async-done(((bf16[512,3,512]{0,2,1:T(8,128)(2,1)}, bf16[512,512]{1,0:T(8,128)(2,1)}, bf16[512,2,2304]{2,1,0:T(2,128)(2,1)}, bf16[2304,512]{1,0:T(8,128)(2,1)}), (bf16[512,3,512]{0,2,1:T(8,128)(2,1)}, bf16[512,512]{1,0:T(8,128)(2,1)}, ...) | async-done | bytes 9175056 | tf_op jit(solution)/shard_map/psum | solution.py:160
  1849.3 41.1 %reduce-scatter.23.cloned.1.call-done = f32[1024,512]{1,0:T(8,128)} async-done(((f32[2048,512]{1,0:T(8,128)}), f32[1024,512]{1,0:T(8,128)}) %reduce-scatter.23.cloned.1.call-update) | async-done | bytes 2097168 | tf_op jit(solution)/shard_map/reduce_scatter | solution.py:58
  1892.9 40.3 %all-reduce = (f32[1024]{0:T(1024)S(1)}, f32[3,1024]{1,0:T(4,128)S(1)}, f32[1024]{0:T(1024)S(1)}) all-reduce(f32[1024]{0:T(1024)S(1)} %dynamic_update_slice.9, f32[3,1024]{1,0:T(4,128)S(1)} %maximum_dynamic-update-slice_fusion, f32[1024]{0:T(1024)S(1)} %dynamic_update_slice.11), channel_id=1, replica_groups=mesh['dp'=8,'row'=2,'col'=2] {'dp','row','col'}, use_global_device_ids=true, to_apply=%region_17.0 | all-reduce | flops 5120 | bytes 40960 | tf_op jit(solution)/shard_map/psum | solution.py:174
  (114 shorter events, 166.0 us)
Async XLA Ops:
  7.2 340.0 %copy-start = (bf16[2304,512]{1,0:T(8,128)(2,1)S(1)}, bf16[2304,512]{1,0:T(8,128)(2,1)}, u32[]{:S(2)}) copy-start(bf16[2304,512]{1,0:T(8,128)(2,1)} %param.16) | copy-start | bytes 7077892
  7.2 45.8 %all-gather.9.cloned.1.call-start = ((), (), s32[]{:S(2)}) async-start(), calls=%async_computation.8 | async-start | bytes 3145728 | tf_op jit(solution)/shard_map/all_gather | solution.py:31
  17.9 189.8 %reduce-scatter.9.cloned.1.call-start = ((), (), s32[]{:S(2)}) async-start(), calls=%async_computation.9 | async-start | bytes 18874368 | tf_op jit(solution)/shard_map/reduce_scatter | solution.py:44
  63.0 149.7 %copy-start.11 = (f32[3,512]{1,0:T(4,128)S(1)}, f32[3,512]{1,0:T(4,128)}, u32[]{:S(2)}) copy-start(f32[3,512]{1,0:T(4,128)} %param.12) | copy-start | bytes 18436
  63.0 190.3 %all-gather.11.cloned.1.call-start = ((), (), s32[]{:S(2)}) async-start(), calls=%async_computation.10 | async-start | bytes 3145728 | tf_op jit(solution)/shard_map/all_gather | solution.py:35
  210.4 3.6 collective-permute-start
  218.1 94.6 %reduce-scatter.11.cloned.1.call-start = ((), (), s32[]{:S(2)}) async-start(), calls=%async_computation.11 | async-start | bytes 6291456 | tf_op jit(solution)/shard_map/reduce_scatter | solution.py:58
  258.1 54.6 %copy-start.1 = (bf16[1024,512]{1,0:T(8,128)(2,1)S(1)}, bf16[1024,512]{1,0:T(8,128)(2,1)}, u32[]{:S(2)}) copy-start(bf16[1024,512]{1,0:T(8,128)(2,1)} %param.9) | copy-start | bytes 3145732
  258.2 89.0 %all-gather.17.cloned.1.call-start = ((), (), s32[]{:S(2)}) async-start(), calls=%async_computation.16 | async-start | bytes 3145728 | tf_op jit(solution)/shard_map/all_gather | solution.py:31
  258.7 62.1 %copy-start.9 = (f32[512]{0:T(512)S(1)}, f32[512]{0:T(512)}, u32[]{:S(2)}) copy-start(f32[512]{0:T(512)} %param.14) | copy-start | bytes 6148
  258.8 123.5 %all-gather.13.cloned.1.call-start = ((), (), s32[]{:S(2)}) async-start(), calls=%async_computation.12 | async-start | bytes 3145728 | tf_op jit(solution)/shard_map/all_gather | solution.py:31
  323.9 272.5 %reduce-scatter.17.cloned.1.call-start = ((), (), s32[]{:S(2)}) async-start(), calls=%async_computation.17 | async-start | bytes 28311552 | tf_op jit(solution)/shard_map/reduce_scatter | solution.py:44
  358.8 653.9 %reduce-scatter.13.cloned.1.call-start = ((), (), s32[]{:S(2)}) async-start(), calls=%async_computation.13 | async-start | bytes 56623104 | tf_op jit(solution)/shard_map/reduce_scatter | solution.py:44
  402.8 852.4 %all-gather.19.cloned.1.call-start = ((), (), s32[]{:S(2)}) async-start(), calls=%async_computation.18 | async-start | bytes 28311552 | tf_op jit(solution)/shard_map/all_gather | solution.py:35
  1030.7 295.5 %reduce-scatter.19.cloned.1.call-start = ((), (), s32[]{:S(2)}) async-start(), calls=%async_computation.19 | async-start | bytes 6291456 | tf_op jit(solution)/shard_map/reduce_scatter | solution.py:58
  1271.7 62.3 %copy-start.4 = (bf16[1024,512]{1,0:T(8,128)(2,1)S(1)}, bf16[1024,512]{1,0:T(8,128)(2,1)}, u32[]{:S(2)}) copy-start(bf16[1024,512]{1,0:T(8,128)(2,1)} %param.17) | copy-start | bytes 3145732
  1271.7 99.4 %all-gather.21.cloned.1.call-start = ((), (), s32[]{:S(2)}) async-start(), calls=%async_computation.20 | async-start | bytes 3145728 | tf_op jit(solution)/shard_map/all_gather | solution.py:31
  1337.8 92.8 %reduce-scatter.21.cloned.1.call-start = ((), (), s32[]{:S(2)}) async-start(), calls=%async_computation.21 | async-start | bytes 6291456 | tf_op jit(solution)/shard_map/reduce_scatter | solution.py:44
  1376.1 174.1 %all-gather.15.cloned.1.call-start = ((), (), s32[]{:S(2)}) async-start(), calls=%async_computation.14 | async-start | bytes 14155776 | tf_op jit(solution)/shard_map/all_gather | solution.py:35
  1376.8 255.7 %all-gather.23.cloned.1.call-start = ((), (), s32[]{:S(2)}) async-start(), calls=%async_computation.22 | async-start | bytes 9437184 | tf_op jit(solution)/shard_map/all_gather | solution.py:35
  1435.9 5.5 collective-permute-start.1
  1448.3 385.5 %all-reduce.4.cloned.1.call-start = ((), (), s32[]{:S(2)}) async-start(), calls=%async_computation.24 | async-start | bytes 18350080 | tf_op jit(solution)/shard_map/psum | solution.py:160
  1643.2 247.2 %reduce-scatter.23.cloned.1.call-start = ((), (), s32[]{:S(2)}) async-start(), calls=%async_computation.23 | async-start | bytes 6291456 | tf_op jit(solution)/shard_map/reduce_scatter | solution.py:58
  1652.2 296.0 %reduce-scatter.15.cloned.1.call-start = ((), (), s32[]{:S(2)}) async-start(), calls=%async_computation.15 | async-start | bytes 6291456 | tf_op jit(solution)/shard_map/reduce_scatter | solution.py:58
  (8 other events, 204.8 us)
Sparse Core Ops, SparseCore 0:
  18.1 34.8 all-gather.8
  63.1 144.5 reduce-scatter.8
  218.2 35.0 all-gather.10
  258.3 54.3 reduce-scatter.10
  314.1 33.0 all-gather.16
  349.2 33.0 all-gather.12
  384.6 211.7 reduce-scatter.16
  598.7 413.9 reduce-scatter.12
  1030.9 224.3 all-gather.18
  1271.8 54.3 reduce-scatter.18
  1337.9 33.0 all-gather.20
  1376.2 54.3 reduce-scatter.20
  1432.2 117.9 all-gather.14
  1552.2 80.3 all-gather.22
  1643.3 190.3 all-reduce.3
  1835.9 54.4 reduce-scatter.22
  1892.6 55.5 reduce-scatter.14
where the time goes:
time: 1970 us; the launch traced here: 1960 us
  waiting for transfers between devices  1660 us (84%)
  matrix products  127 us (6%)
  other arithmetic  74.1 us (4%)
  blocking collectives  61.2 us (3%)
  local copies, waits for them, and re-layouts  23.9 us (1%)
    reduce_scatter x4, waiting for transfers between devices, spread_wide(): lax.psum_scatter(partial_rows(jnp.int32(0), height * lax.axis_size('col')...  808 us
    all_gather x4, waiting for transfers between devices, tokens_by_col(): return lax.all_gather(value, 'col', axis=0, tiled=True)  405 us
    psum x1, waiting for transfers between devices, local(): lax.psum(grad_in.astype(jnp.bfloat16), 'dp').astype(jnp.float32)  171 us
    reduce_scatter x4, waiting for transfers between devices, spread_narrow(): lax.psum_scatter(partial_rows(jnp.int32(0), height * lax.axis_size('row')...  157 us
    all_gather x4, waiting for transfers between devices, tokens_by_row(): return lax.all_gather(value, 'row', axis=0, tiled=True)  107 us
    dot_general x4, matrix products, dense(): return jnp.dot(left, matrix, preferred_element_type=jnp.float32)  45.8 us
    dot_general x4, matrix products, dense(): lax.dot_general(left, matrix, (((1,), (1,)), ((), ())), preferred_element...  41.7 us
    psum x1, blocking collectives, local(): lax.psum((full_one, full_two, full_kernel), ('dp', 'row', 'col'))  40.3 us
  transfers between devices with their start and end apart: 19, of which 19 were waited for; matrix products, arithmetic and copies ran while one was open for 7% of the time, Pallas kernels for 0%

commit v1 on v0

--- a/solution.py
+++ b/solution.py
@@ -32,7 +32,9 @@
 
 
 def tokens_by_col(value):
-    return lax.all_gather(value, "col", axis=0, tiled=True)
+    return jnp.concatenate(
+        lax.all_to_all(jnp.stack([value] * lax.axis_size("col")), "col", 0, 0), axis=0
+    )
 
 
 def spread_wide(gathered, matrix, transposed):

time: 1970 us -> 1930 us (0.980)
  waiting for transfers between devices: 1660 us -> 1340 us
  blocking collectives: 61.2 us -> 300 us
  local copies, waits for them, and re-layouts: 23.9 us -> 56.9 us
    all_gather x4 -> x0, waiting for transfers between devices: 405 us -> none  [tokens_by_col(): return lax.all_gather(value, 'col', axis=0, tiled=True)]
    all_to_all x0 -> x2, blocking collectives: none -> 238 us  [tokens_by_col(): lax.all_to_all(jnp.stack([value] * lax.axis_size('col')), 'col', 0, 0)]
    ppermute x2, waiting for transfers between devices: 5.31 us -> 59.9 us  [shifted(): return lax.ppermute(block, axis, route)]
    dot_general x0 -> x2, local copies, waits for them, and re-layouts: none -> 33.5 us  [grads_of(): lax.dot_general(left, right, (((0,), (0,)), ((), ())), preferred_element_...]
  transfers between devices with their start and end apart: 19 -> 17, of which waited for: 19 -> 16; matrix products, arithmetic and copies ran while one was open for 7% -> 8% of each run, Pallas kernels for 0% -> 0%
where the time goes in v1:
time: 1930 us; the launch traced here: 1920 us
  waiting for transfers between devices  1340 us (69%)
  blocking collectives  300 us (16%)
  matrix products  121 us (6%)
  other arithmetic  75.4 us (4%)
  local copies, waits for them, and re-layouts  56.9 us (3%)
    reduce_scatter x4, waiting for transfers between devices, spread_wide(): lax.psum_scatter(partial_rows(jnp.int32(0), height * lax.axis_size('col')...  828 us
    all_to_all x2, blocking collectives, tokens_by_col(): lax.all_to_all(jnp.stack([value] * lax.axis_size('col')), 'col', 0, 0)  238 us
    psum x1, waiting for transfers between devices, local(): lax.psum(grad_ffn.astype(jnp.bfloat16), 'dp').astype(jnp.float32)  171 us
    reduce_scatter x4, waiting for transfers between devices, spread_narrow(): lax.psum_scatter(partial_rows(jnp.int32(0), height * lax.axis_size('row')...  156 us
    all_gather x4, waiting for transfers between devices, tokens_by_row(): return lax.all_gather(value, 'row', axis=0, tiled=True)  106 us
    ppermute x2, waiting for transfers between devices, shifted(): return lax.ppermute(block, axis, route)  59.9 us
    dot_general x4, matrix products, dense(): return jnp.dot(left, matrix, preferred_element_type=jnp.float32)  44.1 us
    psum x1, blocking collectives, local(): lax.psum((full_one, full_two, full_kernel), ('dp', 'row', 'col'))  40.5 us
  transfers between devices with their start and end apart: 17, of which 16 were waited for; matrix products, arithmetic and copies ran while one was open for 8% of the time, Pallas kernels for 0%

profile of v1, /device:TPU:0, one launch (start us, length us, event | category | flops | bytes accessed | tf_op | source)
XLA Modules:
  0.0 1924.2 jit_solution(8212097030614542255)
XLA Ops:
  20.6 32.4 %all-gather.5.cloned.1.call-done = bf16[2048,512]{1,0:T(8,128)(2,1)} async-done(((bf16[1024,512]{1,0:T(8,128)(2,1)}), bf16[2048,512]{1,0:T(8,128)(2,1)}) %all-gather.5.cloned.1.call-update) | async-done | bytes 2097168 | tf_op jit(solution)/shard_map/all_gather | solution.py:31
  63.1 144.6 %reduce-scatter.9.cloned.1.call-done = f32[1024,1536]{1,0:T(8,128)} async-done(((f32[2048,1536]{1,0:T(8,128)}), f32[1024,1536]{1,0:T(8,128)}) %reduce-scatter.9.cloned.1.call-update) | async-done | bytes 6291472 | tf_op jit(solution)/shard_map/reduce_scatter | solution.py:46
  217.9 27.2 %all_to_all.20 = bf16[2,1024,512]{2,1,0:T(8,128)(2,1)S(1)} all-to-all(bf16[2,1024,512]{2,1,0:T(8,128)(2,1)S(1)} %pad_maximum_fusion.3), channel_id=1, replica_groups=mesh['dp'=8,'row'=2,'col'=2] {'col'}, dimensions={0} | all-to-all | bytes 4194304 | tf_op jit(solution)/shard_map/all_to_all | solution.py:36
  250.5 53.9 %reduce-scatter.11.cloned.1.call-done = f32[1024,512]{1,0:T(8,128)} async-done(((f32[2048,512]{1,0:T(8,128)}), f32[1024,512]{1,0:T(8,128)}) %reduce-scatter.11.cloned.1.call-update) | async-done | bytes 2097168 | tf_op jit(solution)/shard_map/reduce_scatter | solution.py:60
  315.7 23.3 %all-gather.9.cloned.1.call-done = bf16[2048,512]{1,0:T(8,128)(2,1)} async-done(((bf16[1024,512]{1,0:T(8,128)(2,1)}), bf16[2048,512]{1,0:T(8,128)(2,1)}) %all-gather.9.cloned.1.call-update) | async-done | bytes 2097168 | tf_op jit(solution)/shard_map/all_gather | solution.py:31
  339.0 11.5 fusion.37
  356.4 17.7 all-gather.7.cloned.1.call-done
  374.1 20.4 %fusion.35 = f32[2048,4608]{1,0:T(8,128)} fusion(bf16[2048,512]{1,0:T(8,128)(2,1)} %all-gather.7.cloned.1.call-done, bf16[512,4608]{1,0:T(8,128)(2,1)} %bitcast.78), kind=kOutput, calls=%fused_computation.74 | convolution fusion | flops 9663676416 | bytes 44564480 | tf_op jit(solution)/shard_map/dot_general | solution.py:21
  394.6 193.5 %reduce-scatter.17.cloned.1.call-done = f32[1024,2304]{1,0:T(8,128)} async-done(((f32[2048,2304]{1,0:T(8,128)}), f32[1024,2304]{1,0:T(8,128)}) %reduce-scatter.17.cloned.1.call-update) | async-done | bytes 9437200 | tf_op jit(solution)/shard_map/reduce_scatter | solution.py:46
  588.0 416.3 %reduce-scatter.13.cloned.1.call-done = f32[1024,4608]{1,0:T(8,128)} async-done(((f32[2048,4608]{1,0:T(8,128)}), f32[1024,4608]{1,0:T(8,128)}) %reduce-scatter.13.cloned.1.call-update) | async-done | bytes 18874384 | tf_op jit(solution)/shard_map/reduce_scatter | solution.py:46
  1004.3 13.5 fusion.2
  1021.4 211.1 %all_to_all.21 = bf16[2,1024,4608]{2,1,0:T(8,128)(2,1)} all-to-all(bf16[2,1024,4608]{2,1,0:T(8,128)(2,1)S(1)} %maximum_maximum_fusion), channel_id=1, replica_groups=mesh['dp'=8,'row'=2,'col'=2] {'col'}, dimensions={0} | all-to-all | bytes 37748736 | tf_op jit(solution)/shard_map/all_to_all | solution.py:36
  1232.5 15.1 fusion.38
  1247.7 54.4 %reduce-scatter.19.cloned.1.call-done = f32[1024,512]{1,0:T(8,128)} async-done(((f32[2048,512]{1,0:T(8,128)}), f32[1024,512]{1,0:T(8,128)}) %reduce-scatter.19.cloned.1.call-update) | async-done | bytes 2097168 | tf_op jit(solution)/shard_map/reduce_scatter | solution.py:60
  1313.9 33.0 %all-gather.11.cloned.1.call-done = bf16[2048,512]{1,0:T(8,128)(2,1)} async-done(((bf16[1024,512]{1,0:T(8,128)(2,1)}), bf16[2048,512]{1,0:T(8,128)(2,1)}) %all-gather.11.cloned.1.call-update) | async-done | bytes 2097168 | tf_op jit(solution)/shard_map/all_gather | solution.py:31
  1367.8 73.2 %reduce-scatter.21.cloned.1.call-done = f32[1024,512]{1,0:T(8,128)} async-done(((f32[2048,512]{1,0:T(8,128)}), f32[1024,512]{1,0:T(8,128)}) %reduce-scatter.21.cloned.1.call-update) | async-done | bytes 2097168 | tf_op jit(solution)/shard_map/reduce_scatter | solution.py:46
  1447.7 58.6 %collective-permute-done.1 = f32[2,512]{1,0:T(2,128)S(1)} collective-permute-done((f32[2,512]{1,0:T(2,128)S(1)}, f32[2,512]{1,0:T(2,128)S(1)}, u32[]{:S(2)}, u32[]{:S(2)}) %collective-permute-start.1) | collective-permute-done | bytes 4128 | tf_op jit(solution)/shard_map/ppermute | solution.py:13
  1530.2 24.7 %copy.26 = bf16[4608,2048]{1,0:T(8,128)(2,1)} copy(bf16[4608,2048]{0,1:T(8,128)(2,1)} %bitcast.72) | data formatting | bytes 37748736 | tf_op jit(solution)/shard_map/dot_general | solution.py:25
  1554.9 16.1 convolution_convert_fusion
  1573.1 16.8 all-to-all-done.3
  1626.2 171.1 %all-reduce.4.cloned.1.call-done = (bf16[512,2,2304]{2,0,1:T(8,128)(2,1)}, bf16[512,3,512]{2,0,1:T(8,128)(2,1)}, bf16[512,512]{1,0:T(8,128)(2,1)}, bf16[2304,512]{1,0:T(8,128)(2,1)}) async-done(((bf16[512,2,2304]{2,0,1:T(8,128)(2,1)}, bf16[512,3,512]{2,0,1:T(8,128)(2,1)}, bf16[512,512]{1,0:T(8,128)(2,1)}, bf16[2304,512]{1,0:T(8,128)(2,1)}), (bf16[512,2,2304]{2,0,1:T(8,128)(2,1)}, ...) | async-done | bytes 9175056 | tf_op jit(solution)/shard_map/psum | solution.py:164
  1797.2 10.8 copy.28
  1814.2 39.7 %reduce-scatter.23.cloned.1.call-done = f32[1024,512]{1,0:T(8,128)} async-done(((f32[2048,512]{1,0:T(8,128)}), f32[1024,512]{1,0:T(8,128)}) %reduce-scatter.23.cloned.1.call-update) | async-done | bytes 2097168 | tf_op jit(solution)/shard_map/reduce_scatter | solution.py:60
  1856.4 40.5 %all-reduce = (f32[1024]{0:T(1024)S(1)}, f32[3,1024]{1,0:T(4,128)S(1)}, f32[1024]{0:T(1024)S(1)}) all-reduce(f32[1024]{0:T(1024)S(1)} %dynamic_update_slice.9, f32[3,1024]{1,0:T(4,128)S(1)} %maximum_dynamic-update-slice_fusion, f32[1024]{0:T(1024)S(1)} %dynamic_update_slice.11), channel_id=1, replica_groups=mesh['dp'=8,'row'=2,'col'=2] {'dp','row','col'}, use_global_device_ids=true, to_apply=%region_17.0 | all-reduce | flops 5120 | bytes 40960 | tf_op jit(solution)/shard_map/psum | solution.py:176
  (123 shorter events, 190.1 us)
Async XLA Ops:
  7.2 331.8 %copy-start = (bf16[2304,512]{1,0:T(8,128)(2,1)S(1)}, bf16[2304,512]{1,0:T(8,128)(2,1)}, u32[]{:S(2)}) copy-start(bf16[2304,512]{1,0:T(8,128)(2,1)} %param.16) | copy-start | bytes 7077892
  7.2 45.8 %all-gather.5.cloned.1.call-start = ((), (), s32[]{:S(2)}) async-start(), calls=%async_computation.12 | async-start | bytes 3145728 | tf_op jit(solution)/shard_map/all_gather | solution.py:31
  17.9 189.8 %reduce-scatter.9.cloned.1.call-start = ((), (), s32[]{:S(2)}) async-start(), calls=%async_computation.13 | async-start | bytes 18874368 | tf_op jit(solution)/shard_map/reduce_scatter | solution.py:46
  63.0 149.7 %copy-start.16 = (f32[3,512]{1,0:T(4,128)S(1)}, f32[3,512]{1,0:T(4,128)}, u32[]{:S(2)}) copy-start(f32[3,512]{1,0:T(4,128)} %param.12) | copy-start | bytes 18436
  63.0 241.4 %reduce-scatter.11.cloned.1.call-start = ((), (), s32[]{:S(2)}) async-start(), calls=%async_computation.14 | async-start | bytes 6291456 | tf_op jit(solution)/shard_map/reduce_scatter | solution.py:60
  210.4 3.6 collective-permute-start
  249.9 54.6 %copy-start.1 = (bf16[1024,512]{1,0:T(8,128)(2,1)S(1)}, bf16[1024,512]{1,0:T(8,128)(2,1)}, u32[]{:S(2)}) copy-start(bf16[1024,512]{1,0:T(8,128)(2,1)} %param.9) | copy-start | bytes 3145732
  249.9 89.1 %all-gather.9.cloned.1.call-start = ((), (), s32[]{:S(2)}) async-start(), calls=%async_computation.18 | async-start | bytes 3145728 | tf_op jit(solution)/shard_map/all_gather | solution.py:31
  250.5 62.1 %copy-start.14 = (f32[512]{0:T(512)S(1)}, f32[512]{0:T(512)}, u32[]{:S(2)}) copy-start(f32[512]{0:T(512)} %param.14) | copy-start | bytes 6148
  250.5 123.6 %all-gather.7.cloned.1.call-start = ((), (), s32[]{:S(2)}) async-start(), calls=%async_computation.15 | async-start | bytes 3145728 | tf_op jit(solution)/shard_map/all_gather | solution.py:31
  315.7 272.3 %reduce-scatter.17.cloned.1.call-start = ((), (), s32[]{:S(2)}) async-start(), calls=%async_computation.19 | async-start | bytes 28311552 | tf_op jit(solution)/shard_map/reduce_scatter | solution.py:46
  350.5 653.8 %reduce-scatter.13.cloned.1.call-start = ((), (), s32[]{:S(2)}) async-start(), calls=%async_computation.16 | async-start | bytes 56623104 | tf_op jit(solution)/shard_map/reduce_scatter | solution.py:46
  394.5 907.6 %reduce-scatter.19.cloned.1.call-start = ((), (), s32[]{:S(2)}) async-start(), calls=%async_computation.20 | async-start | bytes 6291456 | tf_op jit(solution)/shard_map/reduce_scatter | solution.py:60
  1017.8 214.7 %slice-start = ((s8[4718592]{0:T(1024)(128)(4,1)}), s8[524288]{0:T(1024)(128)(4,1)S(1)}, s32[]{:S(2)}) async-start(s8[4718592]{0:T(1024)(128)(4,1)} %bitcast.79), calls=%async_computation.25 | async-start | bytes 1048576
  1021.4 211.1 %slice-start.1 = ((s8[4718592]{0:T(1024)(128)(4,1)}), s8[4194304]{0:T(1024)(128)(4,1)S(1)}, s32[]{:S(2)}) async-start(s8[4718592]{0:T(1024)(128)(4,1)} %bitcast.79), calls=%async_computation.26 | async-start | bytes 8388608
  1247.6 62.3 %copy-start.7 = (bf16[1024,512]{1,0:T(8,128)(2,1)S(1)}, bf16[1024,512]{1,0:T(8,128)(2,1)}, u32[]{:S(2)}) copy-start(bf16[1024,512]{1,0:T(8,128)(2,1)} %param.17) | copy-start | bytes 3145732
  1247.6 99.3 %all-gather.11.cloned.1.call-start = ((), (), s32[]{:S(2)}) async-start(), calls=%async_computation.21 | async-start | bytes 3145728 | tf_op jit(solution)/shard_map/all_gather | solution.py:31
  1313.7 127.3 %reduce-scatter.21.cloned.1.call-start = ((), (), s32[]{:S(2)}) async-start(), calls=%async_computation.22 | async-start | bytes 6291456 | tf_op jit(solution)/shard_map/reduce_scatter | solution.py:46
  1360.4 153.1 %all-to-all-start.1 = ((bf16[2,1024,2304]{2,1,0:T(8,128)(2,1)}), bf16[2,1024,2304]{2,1,0:T(8,128)(2,1)}, u32[]{:S(2)}, u32[]{:S(2)}) async-start(bf16[2,1024,2304]{2,1,0:T(8,128)(2,1)} %pad_maximum_fusion), calls=%async_computation.4 | async-start | bytes 18874368 | tf_op jit(solution)/shard_map/all_to_all | solution.py:36
  1446.4 59.9 %collective-permute-start.1 = (f32[2,512]{1,0:T(2,128)S(1)}, f32[2,512]{1,0:T(2,128)S(1)}, u32[]{:S(2)}, u32[]{:S(2)}) collective-permute-start(f32[2,512]{1,0:T(2,128)S(1)} %slice.67), channel_id=1, source_target_pairs={{1,0},{3,2},{5,4},{7,6},{9,8},{11,10},{13,12},{15,14},{17,16},{19,... | collective-permute-start | bytes 12296 | tf_op jit(solution)/shard_map/ppermute | solution.py:13
  1513.5 76.3 %all-to-all-start.3 = ((bf16[2,1024,1536]{2,1,0:T(8,128)(2,1)}), bf16[2,1024,1536]{2,1,0:T(8,128)(2,1)}, u32[]{:S(2)}, u32[]{:S(2)}) async-start(bf16[2,1024,1536]{2,1,0:T(8,128)(2,1)} %maximum_maximum_fusion.1), calls=%async_computation.10 | async-start | bytes 12582912 | tf_op jit(solution)/shard_map/all_to_all | solution.py:36
  1519.7 277.5 %all-reduce.4.cloned.1.call-start = ((), (), s32[]{:S(2)}) async-start(), calls=%async_computation.24 | async-start | bytes 18350080 | tf_op jit(solution)/shard_map/psum | solution.py:164
  1606.7 247.2 %reduce-scatter.23.cloned.1.call-start = ((), (), s32[]{:S(2)}) async-start(), calls=%async_computation.23 | async-start | bytes 6291456 | tf_op jit(solution)/shard_map/reduce_scatter | solution.py:60
  1615.4 296.4 %reduce-scatter.15.cloned.1.call-start = ((), (), s32[]{:S(2)}) async-start(), calls=%async_computation.17 | async-start | bytes 6291456 | tf_op jit(solution)/shard_map/reduce_scatter | solution.py:60
  (12 other events, 214.9 us)
Sparse Core Ops, SparseCore 0:
  18.1 34.8 all-gather.4
  63.1 144.5 reduce-scatter.8
  250.0 54.3 reduce-scatter.10
  305.8 33.0 all-gather.8
  340.9 33.0 all-gather.6
  376.2 211.7 reduce-scatter.16
  590.3 413.9 reduce-scatter.12
  1247.7 54.3 reduce-scatter.18
  1313.8 33.0 all-gather.10
  1352.1 88.9 reduce-scatter.20
  1606.8 190.3 all-reduce.3
  1799.4 54.4 reduce-scatter.22
  1856.2 55.6 reduce-scatter.14
